TPU v7x, 256 devices: a whole 4x4x8 slice. The times are simulated.
256 devices in a mesh: row: 8 (over y, core), col: 32 (over x, z).
Axes of the slice: x: 4, y: 4, z: 8, core: 2. Of those that a mesh axis runs over, the one named last changes fastest.
Arguments:
- features: bfloat16 [65536, 512], P(('row', 'col')), may hold values from -6 to 6
- memory: float32 [65536, 512], P(('col', 'row')), may hold values from -1 to 1
- tile_values: bfloat16 [8, 32, 128, 128, 128], P('row', 'col'), as said below
- tile_rows: int32 [8, 32, 128], P('row', 'col'), may hold values from 0 to 15, as said below
- tile_cols: int32 [8, 32, 128], P('row', 'col'), may hold values from 0 to 63
- tile_count: int32 [8, 32], P('row', 'col'), may hold values from 16 to 128, as said below
- conv_weight: bfloat16 [512, 512], replicated, may hold values from -0.25 to 0.25
- conv_bias: float32 [512], replicated, may hold values from -3 to 3
- input_weight: bfloat16 [512, 1536], replicated, may hold values from -0.25 to 0.25
- input_bias: float32 [1536], replicated, may hold values from -3 to 3
- hidden_weight: bfloat16 [512, 1536], replicated, may hold values from -0.25 to 0.25
- hidden_bias: float32 [1536], replicated, may hold values from -3 to 3
Outputs:
- new_memory: float32 [65536, 512], P(('col', 'row'))
Inputs may be any that keep to these rules, and one draw needn't show every extreme that they name: `tile_values`: edge weights are nonnegative. For each device pair (r, c) the 128 pairs (tile_rows, tile_cols) are distinct. `tile_count`: in every draw some device pair has all 128 slots live.
All inputs are finite; a program needn't handle non-finite values.
Results may differ from a plain program's by a relative error of at most 0.017.
Values may be sent and summed in bfloat16 or wider, within the bound.
A program may use at most 128 MiB of HBM per device.

v0:
```python
import jax
import jax.numpy as jnp
from jax import lax
from jax.sharding import PartitionSpec as P

norm_epsilon = 1e-06
tiles_per_pass = 32


def gru_update(message, memory, input_weight, input_bias, hidden_weight, hidden_bias):
    width = memory.shape[1]
    from_input = jnp.dot(message, input_weight, preferred_element_type=jnp.float32) + input_bias
    held = memory.astype(jnp.bfloat16)
    from_memory = jnp.dot(held, hidden_weight, preferred_element_type=jnp.float32) + hidden_bias
    reset = jax.nn.sigmoid(from_input[:, :width] + from_memory[:, :width])
    update = jax.nn.sigmoid(from_input[:, width : 2 * width] + from_memory[:, width : 2 * width])
    candidate = jnp.tanh(from_input[:, 2 * width :] + reset * from_memory[:, 2 * width :])
    return (1.0 - update) * candidate + update * memory


def on_device(
    features,
    memory,
    tile_values,
    tile_rows,
    tile_cols,
    tile_count,
    conv_weight,
    conv_bias,
    input_weight,
    input_bias,
    hidden_weight,
    hidden_bias,
):
    own_rows, width = features.shape
    tile_data = tile_values[0, 0]
    row_ids = tile_rows[0, 0]
    col_ids = tile_cols[0, 0]
    live_count = tile_count[0, 0]
    slot_total = tile_data.shape[0]
    tile_size = tile_data.shape[1]
    row_blocks = own_rows * lax.axis_size("row") // tile_size
    col_blocks = own_rows * lax.axis_size("col") // tile_size
    per_pass = min(tiles_per_pass, slot_total)
    live = jnp.arange(slot_total) < live_count
    column_sums = jnp.sum(tile_data, axis=1, dtype=jnp.float32) * live[:, None]
    picker = ((col_ids[:, None] == jnp.arange(col_blocks)[None, :]) & live[:, None]).astype(
        jnp.float32
    )
    out_terms = jnp.einsum(
        "tb,tq->bq", picker, column_sums, precision=lax.Precision.HIGHEST
    ).reshape(col_blocks * tile_size)
    gathered = lax.all_gather(features, "col", axis=0, tiled=True)
    all_degree = 1.0 + lax.psum(out_terms.astype(jnp.bfloat16), "col").astype(jnp.float32)
    gathered = (gathered.astype(jnp.float32) * lax.rsqrt(all_degree)[:, None]).astype(jnp.bfloat16)
    panel = gathered.reshape(col_blocks, tile_size, width)

    def advance(block_index, summed):
        first_slot = block_index * per_pass
        block_rows = lax.dynamic_slice_in_dim(row_ids, first_slot, per_pass)
        block_cols = lax.dynamic_slice_in_dim(col_ids, first_slot, per_pass)
        block_tiles = lax.dynamic_slice_in_dim(tile_data, first_slot, per_pass)
        block_live = first_slot + jnp.arange(per_pass) < live_count
        block_tiles = jnp.where(block_live[:, None, None], block_tiles, jnp.zeros((), jnp.bfloat16))
        picked = jnp.take(panel, block_cols, axis=0)
        products = jnp.einsum(
            "tpq,tqf->tpf", block_tiles, picked, preferred_element_type=jnp.float32
        )
        return summed.at[block_rows].add(products)

    passes = (live_count + per_pass - 1) // per_pass
    summed = lax.fori_loop(
        0, passes, advance, jnp.zeros((row_blocks, tile_size, width), jnp.float32)
    )
    partial_value = summed.reshape(row_blocks * tile_size, width)
    owned = lax.psum_scatter(
        partial_value.astype(jnp.bfloat16), "row", scatter_dimension=0, tiled=True
    ).astype(jnp.float32)
    normed = (
        owned / jnp.sqrt(jnp.mean(owned * owned, axis=1, keepdims=True) + norm_epsilon)
    ).astype(jnp.bfloat16)
    message = jax.nn.relu(
        jnp.dot(normed, conv_weight, preferred_element_type=jnp.float32) + conv_bias
    ).astype(jnp.bfloat16)
    return gru_update(message, memory, input_weight, input_bias, hidden_weight, hidden_bias)


def solution(mesh):
    placed = (
        P(("row", "col"), None),
        P(("col", "row"), None),
        P("row", "col", None, None, None),
        P("row", "col", None),
        P("row", "col", None),
        P("row", "col"),
        P(),
        P(),
        P(),
        P(),
        P(),
        P(),
    )
    return jax.shard_map(
        on_device, mesh=mesh, in_specs=placed, out_specs=P(("col", "row"), None), check_vma=False
    )
```

profile of v0, /device:TPU:4, one launch (start us, length us, event | category | flops | bytes accessed | tf_op | source)
XLA Modules:
  0.0 344.7 jit_solution(16640008878866599915)
XLA Ops:
  6.5 0.0 copy-start
  6.5 0.0 copy-start.1
  6.5 0.0 all-gather.2.cloned.1.call-start
  6.5 0.7 all-gather.2.cloned.1.call-update
  7.3 0.0 reduce-scatter.2.cloned.1.call-start
  8.0 3.4 convert_reduce_fusion
  11.4 0.0 copy-done.1
  11.4 0.3 fusion.13
  11.7 125.3 %psum.7 = bf16[8192]{0:T(1024)(128)(2,1)S(1)} all-reduce(bf16[8192]{0:T(1024)(128)(2,1)S(1)} %fusion.13), channel_id=1, replica_groups=mesh['row'=8,'col'=32] {'col'}, use_global_device_ids=true, to_apply=%region_1.0 | all-reduce | flops 8192 | bytes 32768 | tf_op jit(solution)/shard_map/psum | solution.py:54
  137.0 0.0 all-gather.2.cloned.1.call-done
  137.1 7.6 %multiply_convert_fusion = bf16[8192,512]{1,0:T(8,128)(2,1)} fusion(bf16[8192,512]{1,0:T(8,128)(2,1)} %all-gather.2.cloned.1.call-done, f32[8192]{0:T(1024)S(1)} %add_rsqrt_fusion), kind=kLoop, calls=%fused_computation.18 | loop fusion | flops 12582912 | bytes 16809984 | tf_op jit(solution)/shard_map/convert_element_type | solution.py:55
  144.7 0.0 copy-start.5
  144.7 2.5 broadcast_in_dim.39
  147.2 0.0 copy-done.5
  147.2 129.4 %while.10 = (s32[]{:T(128)}, f32[16,128,512]{2,1,0:T(8,128)}, s32[]{:T(128)}, s32[128]{0:T(128)S(1)}, s32[]{:T(128)}, /*index=5*/bf16[128,128,128]{2,1,0:T(8,128...) while((s32[]{:T(128)}, f32[16,128,512]{2,1,0:T(8,128)}, ...), condition=%wide.region_4.5_spmd, body=%wide.region_2.4_spmd.sunk | while | flops 541590912 | bytes 47191224 | solution.py:72
  147.2 0.7 compare_and_fusion.2
  147.9 6.1 %gather_fusion = bf16[32,128,512]{2,1,0:T(8,128)(2,1)} fusion(bf16[64,128,512]{2,1,0:T(8,128)(2,1)} %get-tuple-element.157, s32[1024]{0:T(1024)S(1)} %pad_clamp_fusion.2), kind=kCustom, calls=%fused_computation.clone.1 | custom fusion | bytes 8388736 | tf_op jit(solution)/shard_map/while/body/jit(_take)/gather | solution.py:65
  154.1 7.0 %fusion.51 = f32[32,128,512]{2,1,0:T(8,128)} fusion(bf16[32,128,512]{2,1,0:T(8,128)(2,1)} %gather_fusion, pred[32]{0:T(512)(128)(4,1)S(1)} %get-tuple-element.124, bf16[128,128,128]{2,1,0:T(8,128)(2,1)} %get-tuple-element.155, s32[]{:T(128)S(6)} %select_n.41, pred[32]{0:T(512)(128)(4,1)S(1)} %get-tuple-element.125), kind=kOutput, calls=%fused_computation.2.clone.1 | convolution fusion | flops 539492352 | bytes 13631556 | tf_op jit(solution)/shard_map/while/body/tpq,tqf->tpf/dot_general | solution.py:66
  161.1 0.1 compare_select_fusion.4
  161.2 18.2 %scatter_fusion = f32[16,128,512]{2,1,0:T(8,128)} fusion(f32[16,128,512]{2,1,0:T(8,128)} %get-tuple-element.139, s32[32]{0:T(128)S(1)} %compare_select_fusion.4, f32[32,128,512]{2,1,0:T(8,128)} %fusion.51), kind=kCustom, calls=%fused_computation.1.clone.1 | custom fusion | flops 2097152 | bytes 25165952 | tf_op jit(solution)/shard_map/while/body/scatter-add | solution.py:69
  179.4 0.7 compare_and_fusion.2
  180.1 6.1 %gather_fusion = bf16[32,128,512]{2,1,0:T(8,128)(2,1)} fusion(bf16[64,128,512]{2,1,0:T(8,128)(2,1)} %get-tuple-element.157, s32[1024]{0:T(1024)S(1)} %pad_clamp_fusion.2), kind=kCustom, calls=%fused_computation.clone.1 | custom fusion | bytes 8388736 | tf_op jit(solution)/shard_map/while/body/jit(_take)/gather | solution.py:65
  186.2 7.0 %fusion.51 = f32[32,128,512]{2,1,0:T(8,128)} fusion(bf16[32,128,512]{2,1,0:T(8,128)(2,1)} %gather_fusion, pred[32]{0:T(512)(128)(4,1)S(1)} %get-tuple-element.124, bf16[128,128,128]{2,1,0:T(8,128)(2,1)} %get-tuple-element.155, s32[]{:T(128)S(6)} %select_n.41, pred[32]{0:T(512)(128)(4,1)S(1)} %get-tuple-element.125), kind=kOutput, calls=%fused_computation.2.clone.1 | convolution fusion | flops 539492352 | bytes 13631556 | tf_op jit(solution)/shard_map/while/body/tpq,tqf->tpf/dot_general | solution.py:66
  193.3 0.1 compare_select_fusion.4
  193.4 18.4 %scatter_fusion = f32[16,128,512]{2,1,0:T(8,128)} fusion(f32[16,128,512]{2,1,0:T(8,128)} %get-tuple-element.139, s32[32]{0:T(128)S(1)} %compare_select_fusion.4, f32[32,128,512]{2,1,0:T(8,128)} %fusion.51), kind=kCustom, calls=%fused_computation.1.clone.1 | custom fusion | flops 2097152 | bytes 25165952 | tf_op jit(solution)/shard_map/while/body/scatter-add | solution.py:69
  211.8 0.7 compare_and_fusion.2
  212.5 6.1 %gather_fusion = bf16[32,128,512]{2,1,0:T(8,128)(2,1)} fusion(bf16[64,128,512]{2,1,0:T(8,128)(2,1)} %get-tuple-element.157, s32[1024]{0:T(1024)S(1)} %pad_clamp_fusion.2), kind=kCustom, calls=%fused_computation.clone.1 | custom fusion | bytes 8388736 | tf_op jit(solution)/shard_map/while/body/jit(_take)/gather | solution.py:65
  218.6 7.0 %fusion.51 = f32[32,128,512]{2,1,0:T(8,128)} fusion(bf16[32,128,512]{2,1,0:T(8,128)(2,1)} %gather_fusion, pred[32]{0:T(512)(128)(4,1)S(1)} %get-tuple-element.124, bf16[128,128,128]{2,1,0:T(8,128)(2,1)} %get-tuple-element.155, s32[]{:T(128)S(6)} %select_n.41, pred[32]{0:T(512)(128)(4,1)S(1)} %get-tuple-element.125), kind=kOutput, calls=%fused_computation.2.clone.1 | convolution fusion | flops 539492352 | bytes 13631556 | tf_op jit(solution)/shard_map/while/body/tpq,tqf->tpf/dot_general | solution.py:66
  225.7 0.1 compare_select_fusion.4
  225.7 18.5 %scatter_fusion = f32[16,128,512]{2,1,0:T(8,128)} fusion(f32[16,128,512]{2,1,0:T(8,128)} %get-tuple-element.139, s32[32]{0:T(128)S(1)} %compare_select_fusion.4, f32[32,128,512]{2,1,0:T(8,128)} %fusion.51), kind=kCustom, calls=%fused_computation.1.clone.1 | custom fusion | flops 2097152 | bytes 25165952 | tf_op jit(solution)/shard_map/while/body/scatter-add | solution.py:69
  244.2 0.7 compare_and_fusion.2
  244.9 6.1 %gather_fusion = bf16[32,128,512]{2,1,0:T(8,128)(2,1)} fusion(bf16[64,128,512]{2,1,0:T(8,128)(2,1)} %get-tuple-element.157, s32[1024]{0:T(1024)S(1)} %pad_clamp_fusion.2), kind=kCustom, calls=%fused_computation.clone.1 | custom fusion | bytes 8388736 | tf_op jit(solution)/shard_map/while/body/jit(_take)/gather | solution.py:65
  251.1 7.0 %fusion.51 = f32[32,128,512]{2,1,0:T(8,128)} fusion(bf16[32,128,512]{2,1,0:T(8,128)(2,1)} %gather_fusion, pred[32]{0:T(512)(128)(4,1)S(1)} %get-tuple-element.124, bf16[128,128,128]{2,1,0:T(8,128)(2,1)} %get-tuple-element.155, s32[]{:T(128)S(6)} %select_n.41, pred[32]{0:T(512)(128)(4,1)S(1)} %get-tuple-element.125), kind=kOutput, calls=%fused_computation.2.clone.1 | convolution fusion | flops 539492352 | bytes 13631556 | tf_op jit(solution)/shard_map/while/body/tpq,tqf->tpf/dot_general | solution.py:66
  258.1 0.1 compare_select_fusion.4
  258.2 18.4 %scatter_fusion = f32[16,128,512]{2,1,0:T(8,128)} fusion(f32[16,128,512]{2,1,0:T(8,128)} %get-tuple-element.139, s32[32]{0:T(128)S(1)} %compare_select_fusion.4, f32[32,128,512]{2,1,0:T(8,128)} %fusion.51), kind=kCustom, calls=%fused_computation.1.clone.1 | custom fusion | flops 2097152 | bytes 25165952 | tf_op jit(solution)/shard_map/while/body/scatter-add | solution.py:69
  276.6 0.0 copy-start.2
  276.6 3.8 %convert_element_type.52 = bf16[16,128,512]{2,1,0:T(8,128)(2,1)} convert(f32[16,128,512]{2,1,0:T(8,128)} %get-tuple-element.48) | non-fusion elementwise | flops 1048576 | bytes 6291456 | tf_op jit(solution)/shard_map/convert_element_type | solution.py:77
  280.4 0.0 copy-start.3
  280.4 0.0 reduce-scatter.2.cloned.1.call-update
  280.5 0.0 copy-done
  280.5 0.0 copy-done.2
  280.5 1.6 convolution_add_fusion
  282.1 48.2 %reduce-scatter.2.cloned.1.call-done = bf16[256,512]{1,0:T(8,128)(2,1)} async-done(((bf16[2048,512]{1,0:T(8,128)(2,1)}), bf16[256,512]{1,0:T(8,128)(2,1)}) %reduce-scatter.2.cloned.1.call-update) | async-done | bytes 262160 | tf_op jit(solution)/shard_map/reduce_scatter | solution.py:76
  330.3 1.1 fusion.14
  331.4 0.0 copy-done.3
  331.4 0.0 copy-done.4
  331.5 3.7 %convolution_add_fusion.1 = f32[256,1536]{1,0:T(8,128)} fusion(bf16[512,1536]{1,0:T(8,128)(2,1)} %param.22, bf16[512,512]{1,0:T(8,128)(2,1)} %param.20, f32[1536]{0:T(1024)S(1)} %copy-done.3, bf16[256,512]{1,0:T(8,128)(2,1)} %reduce-scatter.2.cloned.1.call-done, f32[512]{0:T(512)S(1)} %copy-done.4, f32[256]{0:T(256)S(1)} %add_sqrt_fusion), kind=kOutput, calls=%fused_computation.21 | convolution fusion | flops 538050560 | bytes 3941376 | tf_op jit(solution)/shard_map/dot_general | solution.py:12
  335.1 2.8 fusion.19
  (8 shorter events, 0.1 us)
Async XLA Ops:
  6.5 273.9 %copy-start = (bf16[512,1536]{1,0:T(8,128)(2,1)S(1)}, bf16[512,1536]{1,0:T(8,128)(2,1)}, u32[]{:S(2)}) copy-start(bf16[512,1536]{1,0:T(8,128)(2,1)} %param.24) | copy-start | bytes 4718596
  6.5 4.9 %copy-start.1 = (s32[1,1,128]{2,1,0:T(1,128)S(1)}, s32[1,1,128]{2,1,0:T(1,128)}, u32[]{:S(2)}) copy-start(s32[1,1,128]{2,1,0:T(1,128)} %param.18) | copy-start | bytes 1540
  6.5 130.5 %all-gather.2.cloned.1.call-start = ((), (), s32[]{:S(2)}) async-start(), calls=%async_computation.1 | async-start | bytes 8650752 | tf_op jit(solution)/shard_map/all_gather | solution.py:53
  7.3 323.1 %reduce-scatter.2.cloned.1.call-start = ((), (), s32[]{:S(2)}) async-start(), calls=%async_computation.2 | async-start | bytes 2359296 | tf_op jit(solution)/shard_map/reduce_scatter | solution.py:76
  144.7 2.5 copy-start.5
  276.6 3.9 %copy-start.2 = (f32[1536]{0:T(1024)S(1)}, f32[1536]{0:T(1024)}, u32[]{:S(2)}) copy-start(f32[1536]{0:T(1024)} %param.25) | copy-start | bytes 18436
  280.4 51.0 %copy-start.3 = (f32[1536]{0:T(1024)S(1)}, f32[1536]{0:T(1024)}, u32[]{:S(2)}) copy-start(f32[1536]{0:T(1024)} %param.23) | copy-start | bytes 18436
  280.4 51.0 %copy-start.4 = (f32[512]{0:T(512)S(1)}, f32[512]{0:T(512)}, u32[]{:S(2)}) copy-start(f32[512]{0:T(512)} %param.21) | copy-start | bytes 6148
Sparse Core Ops, SparseCore 0:
  10.0 100.8 all-gather.1
  280.6 49.7 reduce-scatter.1
where the time goes:
time: 345 us
  blocking collectives  125 us (36%)
  other arithmetic  95.5 us (28%)
  waiting for transfers between devices  49 us (14%)
  matrix products  33.7 us (10%)
  local copies, waits for them, and re-layouts  27.1 us (8%)
  between operations  14.2 us (4%)
    psum x1, blocking collectives, on_device(): lax.psum(out_terms.astype(jnp.bfloat16), 'col').astype(jnp.float32)  125 us
    scatter-add x4, other arithmetic, advance(): return summed.at[block_rows].add(products)  73.5 us
    reduce_scatter x1, waiting for transfers between devices, on_device(): lax.psum_scatter(partial_value.astype(jnp.bfloat16), 'row', scatter_dimen...  48.2 us
    dot_general x4, matrix products, advance(): jnp.einsum('tpq,tqf->tpf', block_tiles, picked, preferred_element_type=jn...  28.1 us
    gather x4, local copies, waits for them, and re-layouts, advance(): picked = jnp.take(panel, block_cols, axis=0)  24.5 us
    convert_element_type x1, other arithmetic, on_device(): (gathered.astype(jnp.float32) * lax.rsqrt(all_degree)[:, None]).astype(jn...  7.63 us
  transfers between devices with their start and end apart: 2, of which 1 were waited for; matrix products, arithmetic and copies ran while one was open for 2% of the time, Pallas kernels for 0%

commit v1 on v0

--- a/solution.py
+++ b/solution.py
@@ -51,7 +51,9 @@
         "tb,tq->bq", picker, column_sums, precision=lax.Precision.HIGHEST
     ).reshape(col_blocks * tile_size)
     gathered = lax.all_gather(features, "col", axis=0, tiled=True)
-    all_degree = 1.0 + lax.psum(out_terms.astype(jnp.bfloat16), "col").astype(jnp.float32)
+    all_degree = 1.0 + jnp.sum(
+        lax.all_gather(out_terms.astype(jnp.bfloat16), "col"), axis=0
+    ).astype(jnp.float32)
     gathered = (gathered.astype(jnp.float32) * lax.rsqrt(all_degree)[:, None]).astype(jnp.bfloat16)
     panel = gathered.reshape(col_blocks, tile_size, width)
 

time: 345 us -> 303 us (0.88)
  blocking collectives: 125 us -> 53.2 us
  waiting for transfers between devices: 49 us -> 77.1 us
    psum x1 -> x0, blocking collectives: 125 us -> none  [on_device(): lax.psum(out_terms.astype(jnp.bfloat16), 'col').astype(jnp.float32)]
    all_gather x0 -> x1, blocking collectives: none -> 53.2 us  [on_device(): lax.all_gather(out_terms.astype(jnp.bfloat16), 'col')]
    all_gather x1, waiting for transfers between devices: 0.02 us -> 44.2 us  [on_device(): gathered = lax.all_gather(features, 'col', axis=0, tiled=True)]
    reduce_scatter x1, waiting for transfers between devices: 48.2 us -> 32.1 us  [on_device(): lax.psum_scatter(partial_value.astype(jnp.bfloat16), 'row', scatter_dimen...]
  transfers between devices with their start and end apart: 2 -> 2, of which waited for: 1 -> 2; matrix products, arithmetic and copies ran while one was open for 2% -> 2% of each run, Pallas kernels for 0% -> 0%
where the time goes in v1:
time: 303 us; the launch traced here: 302 us
  other arithmetic  96.4 us (32%)
  waiting for transfers between devices  77.1 us (25%)
  blocking collectives  53.2 us (18%)
  matrix products  33.7 us (11%)
  local copies, waits for them, and re-layouts  27.1 us (9%)
  between operations  14.2 us (5%)
    scatter-add x4, other arithmetic, advance(): return summed.at[block_rows].add(products)  73.5 us
    all_gather x1, blocking collectives, on_device(): lax.all_gather(out_terms.astype(jnp.bfloat16), 'col')  53.2 us
    all_gather x1, waiting for transfers between devices, on_device(): gathered = lax.all_gather(features, 'col', axis=0, tiled=True)  44.2 us
    reduce_scatter x1, waiting for transfers between devices, on_device(): lax.psum_scatter(partial_value.astype(jnp.bfloat16), 'row', scatter_dimen...  32.1 us
    dot_general x4, matrix products, advance(): jnp.einsum('tpq,tqf->tpf', block_tiles, picked, preferred_element_type=jn...  28.1 us
    gather x4, local copies, waits for them, and re-layouts, advance(): picked = jnp.take(panel, block_cols, axis=0)  24.5 us
    convert_element_type x1, other arithmetic, on_device(): (gathered.astype(jnp.float32) * lax.rsqrt(all_degree)[:, None]).astype(jn...  7.63 us
  transfers between devices with their start and end apart: 2, of which 2 were waited for; matrix products, arithmetic and copies ran while one was open for 2% of the time, Pallas kernels for 0%

profile of v1, /device:TPU:4, one launch (start us, length us, event | category | flops | bytes accessed | tf_op | source)
XLA Modules:
  0.0 301.8 jit_solution(13938603511683014078)
XLA Ops:
  6.5 0.0 copy-start
  6.5 0.0 copy-start.1
  6.5 0.0 all-gather.3.cloned.1.call-start
  6.5 0.7 all-gather.3.cloned.1.call-update
  7.3 0.0 reduce-scatter.2.cloned.1.call-start
  8.0 3.4 %convert_reduce_fusion = f32[128,128]{1,0:T(8,128)S(1)} fusion(bf16[1,1,128,128,128]{4,3,2,1,0:T(8,128)(2,1)} %param.16), kind=kLoop, calls=%fused_computation.19 | loop fusion | flops 4177920 | bytes 4259840 | tf_op jit(solution)/shard_map/reduce_sum | solution.py:46
  11.4 0.0 copy-done.1
  11.4 0.3 convolution_convert_fusion
  11.8 53.2 %all-gather = bf16[32,1,8192]{2,1,0:T(2,128)(2,1)S(1)} all-gather(bf16[1,1,8192]{2,1,0:T(2,128)(2,1)S(1)} %reshape.71), channel_id=1, replica_groups=mesh['row'=8,'col'=32] {'col'}, dimensions={0}, use_global_device_ids=true | all-gather | bytes 540672 | tf_op jit(solution)/shard_map/all_gather | solution.py:55
  65.0 1.0 reduce_sum.31
  66.0 44.2 %all-gather.3.cloned.1.call-done = bf16[8192,512]{1,0:T(8,128)(2,1)} async-done(((bf16[256,512]{1,0:T(8,128)(2,1)}), bf16[8192,512]{1,0:T(8,128)(2,1)}) %all-gather.3.cloned.1.call-update) | async-done | bytes 8388624 | tf_op jit(solution)/shard_map/all_gather | solution.py:53
  110.3 7.6 %multiply_convert_fusion = bf16[8192,512]{1,0:T(8,128)(2,1)} fusion(bf16[8192,512]{1,0:T(8,128)(2,1)} %all-gather.3.cloned.1.call-done, f32[8192]{0:T(1024)S(1)} %add_rsqrt_fusion), kind=kLoop, calls=%fused_computation.18 | loop fusion | flops 12582912 | bytes 16809984 | tf_op jit(solution)/shard_map/convert_element_type | solution.py:57
  117.9 0.0 copy-start.5
  117.9 2.5 broadcast_in_dim.39
  120.4 0.0 copy-done.5
  120.4 129.4 %while.10 = (s32[]{:T(128)}, f32[16,128,512]{2,1,0:T(8,128)}, s32[]{:T(128)}, s32[128]{0:T(128)S(1)}, s32[]{:T(128)}, /*index=5*/bf16[128,128,128]{2,1,0:T(8,128...) while((s32[]{:T(128)}, f32[16,128,512]{2,1,0:T(8,128)}, ...), condition=%wide.region_4.5_spmd, body=%wide.region_2.4_spmd.sunk | while | flops 541590912 | bytes 47191224 | solution.py:74
  120.4 0.7 compare_and_fusion.2
  121.1 6.1 %gather_fusion = bf16[32,128,512]{2,1,0:T(8,128)(2,1)} fusion(bf16[64,128,512]{2,1,0:T(8,128)(2,1)} %get-tuple-element.157, s32[1024]{0:T(1024)S(1)} %pad_clamp_fusion.2), kind=kCustom, calls=%fused_computation.clone.1 | custom fusion | bytes 8388736 | tf_op jit(solution)/shard_map/while/body/jit(_take)/gather | solution.py:67
  127.3 7.0 %fusion.50 = f32[32,128,512]{2,1,0:T(8,128)} fusion(bf16[32,128,512]{2,1,0:T(8,128)(2,1)} %gather_fusion, pred[32]{0:T(512)(128)(4,1)S(1)} %get-tuple-element.124, bf16[128,128,128]{2,1,0:T(8,128)(2,1)} %get-tuple-element.155, s32[]{:T(128)S(6)} %select_n.41, pred[32]{0:T(512)(128)(4,1)S(1)} %get-tuple-element.125), kind=kOutput, calls=%fused_computation.2.clone.1 | convolution fusion | flops 539492352 | bytes 13631556 | tf_op jit(solution)/shard_map/while/body/tpq,tqf->tpf/dot_general | solution.py:68
  134.3 0.1 compare_select_fusion.4
  134.4 18.2 %scatter_fusion = f32[16,128,512]{2,1,0:T(8,128)} fusion(f32[16,128,512]{2,1,0:T(8,128)} %get-tuple-element.139, s32[32]{0:T(128)S(1)} %compare_select_fusion.4, f32[32,128,512]{2,1,0:T(8,128)} %fusion.50), kind=kCustom, calls=%fused_computation.1.clone.1 | custom fusion | flops 2097152 | bytes 25165952 | tf_op jit(solution)/shard_map/while/body/scatter-add | solution.py:71
  152.6 0.7 compare_and_fusion.2
  153.3 6.1 %gather_fusion = bf16[32,128,512]{2,1,0:T(8,128)(2,1)} fusion(bf16[64,128,512]{2,1,0:T(8,128)(2,1)} %get-tuple-element.157, s32[1024]{0:T(1024)S(1)} %pad_clamp_fusion.2), kind=kCustom, calls=%fused_computation.clone.1 | custom fusion | bytes 8388736 | tf_op jit(solution)/shard_map/while/body/jit(_take)/gather | solution.py:67
  159.4 7.0 %fusion.50 = f32[32,128,512]{2,1,0:T(8,128)} fusion(bf16[32,128,512]{2,1,0:T(8,128)(2,1)} %gather_fusion, pred[32]{0:T(512)(128)(4,1)S(1)} %get-tuple-element.124, bf16[128,128,128]{2,1,0:T(8,128)(2,1)} %get-tuple-element.155, s32[]{:T(128)S(6)} %select_n.41, pred[32]{0:T(512)(128)(4,1)S(1)} %get-tuple-element.125), kind=kOutput, calls=%fused_computation.2.clone.1 | convolution fusion | flops 539492352 | bytes 13631556 | tf_op jit(solution)/shard_map/while/body/tpq,tqf->tpf/dot_general | solution.py:68
  166.5 0.1 compare_select_fusion.4
  166.6 18.4 %scatter_fusion = f32[16,128,512]{2,1,0:T(8,128)} fusion(f32[16,128,512]{2,1,0:T(8,128)} %get-tuple-element.139, s32[32]{0:T(128)S(1)} %compare_select_fusion.4, f32[32,128,512]{2,1,0:T(8,128)} %fusion.50), kind=kCustom, calls=%fused_computation.1.clone.1 | custom fusion | flops 2097152 | bytes 25165952 | tf_op jit(solution)/shard_map/while/body/scatter-add | solution.py:71
  185.0 0.7 compare_and_fusion.2
  185.7 6.1 %gather_fusion = bf16[32,128,512]{2,1,0:T(8,128)(2,1)} fusion(bf16[64,128,512]{2,1,0:T(8,128)(2,1)} %get-tuple-element.157, s32[1024]{0:T(1024)S(1)} %pad_clamp_fusion.2), kind=kCustom, calls=%fused_computation.clone.1 | custom fusion | bytes 8388736 | tf_op jit(solution)/shard_map/while/body/jit(_take)/gather | solution.py:67
  191.8 7.0 %fusion.50 = f32[32,128,512]{2,1,0:T(8,128)} fusion(bf16[32,128,512]{2,1,0:T(8,128)(2,1)} %gather_fusion, pred[32]{0:T(512)(128)(4,1)S(1)} %get-tuple-element.124, bf16[128,128,128]{2,1,0:T(8,128)(2,1)} %get-tuple-element.155, s32[]{:T(128)S(6)} %select_n.41, pred[32]{0:T(512)(128)(4,1)S(1)} %get-tuple-element.125), kind=kOutput, calls=%fused_computation.2.clone.1 | convolution fusion | flops 539492352 | bytes 13631556 | tf_op jit(solution)/shard_map/while/body/tpq,tqf->tpf/dot_general | solution.py:68
  198.9 0.1 compare_select_fusion.4
  198.9 18.5 %scatter_fusion = f32[16,128,512]{2,1,0:T(8,128)} fusion(f32[16,128,512]{2,1,0:T(8,128)} %get-tuple-element.139, s32[32]{0:T(128)S(1)} %compare_select_fusion.4, f32[32,128,512]{2,1,0:T(8,128)} %fusion.50), kind=kCustom, calls=%fused_computation.1.clone.1 | custom fusion | flops 2097152 | bytes 25165952 | tf_op jit(solution)/shard_map/while/body/scatter-add | solution.py:71
  217.4 0.7 compare_and_fusion.2
  218.1 6.1 %gather_fusion = bf16[32,128,512]{2,1,0:T(8,128)(2,1)} fusion(bf16[64,128,512]{2,1,0:T(8,128)(2,1)} %get-tuple-element.157, s32[1024]{0:T(1024)S(1)} %pad_clamp_fusion.2), kind=kCustom, calls=%fused_computation.clone.1 | custom fusion | bytes 8388736 | tf_op jit(solution)/shard_map/while/body/jit(_take)/gather | solution.py:67
  224.3 7.0 %fusion.50 = f32[32,128,512]{2,1,0:T(8,128)} fusion(bf16[32,128,512]{2,1,0:T(8,128)(2,1)} %gather_fusion, pred[32]{0:T(512)(128)(4,1)S(1)} %get-tuple-element.124, bf16[128,128,128]{2,1,0:T(8,128)(2,1)} %get-tuple-element.155, s32[]{:T(128)S(6)} %select_n.41, pred[32]{0:T(512)(128)(4,1)S(1)} %get-tuple-element.125), kind=kOutput, calls=%fused_computation.2.clone.1 | convolution fusion | flops 539492352 | bytes 13631556 | tf_op jit(solution)/shard_map/while/body/tpq,tqf->tpf/dot_general | solution.py:68
  231.3 0.1 compare_select_fusion.4
  231.4 18.4 %scatter_fusion = f32[16,128,512]{2,1,0:T(8,128)} fusion(f32[16,128,512]{2,1,0:T(8,128)} %get-tuple-element.139, s32[32]{0:T(128)S(1)} %compare_select_fusion.4, f32[32,128,512]{2,1,0:T(8,128)} %fusion.50), kind=kCustom, calls=%fused_computation.1.clone.1 | custom fusion | flops 2097152 | bytes 25165952 | tf_op jit(solution)/shard_map/while/body/scatter-add | solution.py:71
  249.8 0.0 copy-start.2
  249.8 3.8 %convert_element_type.65 = bf16[16,128,512]{2,1,0:T(8,128)(2,1)} convert(f32[16,128,512]{2,1,0:T(8,128)} %get-tuple-element.48) | non-fusion elementwise | flops 1048576 | bytes 6291456 | tf_op jit(solution)/shard_map/convert_element_type | solution.py:79
  253.7 0.0 reduce-scatter.2.cloned.1.call-update
  253.7 0.0 copy-done
  253.7 0.0 copy-done.2
  253.7 1.6 convolution_add_fusion
  255.3 32.1 %reduce-scatter.2.cloned.1.call-done = bf16[256,512]{1,0:T(8,128)(2,1)} async-done(((bf16[2048,512]{1,0:T(8,128)(2,1)}), bf16[256,512]{1,0:T(8,128)(2,1)}) %reduce-scatter.2.cloned.1.call-update) | async-done | bytes 262160 | tf_op jit(solution)/shard_map/reduce_scatter | solution.py:78
  287.4 1.1 fusion.13
  288.5 0.0 copy-done.3
  288.5 0.0 copy-done.4
  288.5 3.7 %convolution_add_fusion.1 = f32[256,1536]{1,0:T(8,128)} fusion(bf16[512,1536]{1,0:T(8,128)(2,1)} %param.22, bf16[512,512]{1,0:T(8,128)(2,1)} %param.20, f32[1536]{0:T(1024)S(1)} %copy-done.3, bf16[256,512]{1,0:T(8,128)(2,1)} %reduce-scatter.2.cloned.1.call-done, f32[512]{0:T(512)S(1)} %copy-done.4, f32[256]{0:T(256)S(1)} %add_sqrt_fusion), kind=kOutput, calls=%fused_computation.21 | convolution fusion | flops 538050560 | bytes 3941376 | tf_op jit(solution)/shard_map/dot_general | solution.py:12
  292.2 2.8 fusion.18
  (10 shorter events, 0.1 us)
Async XLA Ops:
  6.5 247.1 %copy-start = (bf16[512,1536]{1,0:T(8,128)(2,1)S(1)}, bf16[512,1536]{1,0:T(8,128)(2,1)}, u32[]{:S(2)}) copy-start(bf16[512,1536]{1,0:T(8,128)(2,1)} %param.24) | copy-start | bytes 4718596
  6.5 4.9 %copy-start.1 = (s32[1,1,128]{2,1,0:T(1,128)S(1)}, s32[1,1,128]{2,1,0:T(1,128)}, u32[]{:S(2)}) copy-start(s32[1,1,128]{2,1,0:T(1,128)} %param.18) | copy-start | bytes 1540
  6.5 103.7 %all-gather.3.cloned.1.call-start = ((), (), s32[]{:S(2)}) async-start(), calls=%async_computation.1 | async-start | bytes 8650752 | tf_op jit(solution)/shard_map/all_gather | solution.py:53
  7.3 280.2 %reduce-scatter.2.cloned.1.call-start = ((), (), s32[]{:S(2)}) async-start(), calls=%async_computation.2 | async-start | bytes 2359296 | tf_op jit(solution)/shard_map/reduce_scatter | solution.py:78
  117.9 2.5 copy-start.5
  249.8 3.9 %copy-start.2 = (f32[1536]{0:T(1024)S(1)}, f32[1536]{0:T(1024)}, u32[]{:S(2)}) copy-start(f32[1536]{0:T(1024)} %param.25) | copy-start | bytes 18436
  253.6 34.9 %copy-start.3 = (f32[1536]{0:T(1024)S(1)}, f32[1536]{0:T(1024)}, u32[]{:S(2)}) copy-start(f32[1536]{0:T(1024)} %param.23) | copy-start | bytes 18436
  253.6 34.9 %copy-start.4 = (f32[512]{0:T(512)S(1)}, f32[512]{0:T(512)}, u32[]{:S(2)}) copy-start(f32[512]{0:T(512)} %param.21) | copy-start | bytes 6148
Sparse Core Ops, SparseCore 0:
  10.0 100.2 all-gather.2
  253.8 33.5 reduce-scatter.1
